TPU v7x, 128 devices: a whole 4x4x4 slice. The times are simulated.
128 devices in a mesh: req: 8 (over z, core), wide: 16 (over x, y).
Axes of the slice: x: 4, y: 4, z: 4, core: 2. Of those that a mesh axis runs over, the one named last changes fastest.
Arguments:
- queries: bfloat16 [16384, 3072], P(('req', 'wide'))
- suffix_latent: bfloat16 [16384, 512], P(('req', 'wide')), may hold values from -6 to 6
- suffix_rope: bfloat16 [64, 16384], P(None, ('req', 'wide')), may hold values from -6 to 6
- residual: bfloat16 [16384, 2048], P(('req', 'wide')), may hold values from -3 to 3
- prefix_latent: bfloat16 [8, 2, 2048, 512], P('req', None, 'wide'), may hold values from -6 to 6
- prefix_rope: bfloat16 [8, 2, 64, 2048], P('req', None, None, 'wide')
- suffix_lengths: int32 [128, 4], P(('req', 'wide')), may hold values from 1 to 64, 128 in all within a row
- prefix_ids: int32 [128, 4], P(('req', 'wide')), may hold values from 0 to 1
- w_ukv: bfloat16 [512, 4096], replicated, may hold values from -0.25 to 0.25
- w_out: bfloat16 [2048, 2048], replicated, may hold values from -0.5 to 0.5
- norm_gain: bfloat16 [2048], replicated, may hold values from 0.099609375 to 1.8984375
- expert_ids: int32 [16384, 6], P(('req', 'wide')), may hold values from 0 to 63, all different within a row; in each aligned block of 128 rows (0 to 127, 128 to 255, ...) at most 13 rows name the same one
- gate_values: float32 [16384, 6], P(('req', 'wide')), may hold values from 0.05 to 0.45
- expert_gate_up: bfloat16 [128, 2048, 1408], P(('req', 'wide')), may hold values from -0.125 to 0.125
- expert_down: bfloat16 [128, 704, 2048], P(('req', 'wide')), may hold values from -0.15625 to 0.15625
Outputs:
- layer_out: bfloat16 [16384, 2048], P(('req', 'wide'))
Inputs may be any that keep to these rules, and one draw needn't show every extreme that they name: `suffix_lengths`: row b gives, in order, the lengths of the 4 requests that make up tokens b * 128 to (b + 1) * 128 - 1; each row sums to 128 and its largest entry is 64. `expert_ids`: a token's 6 experts differ; among the 128 tokens of one device no expert is named more than 13 times, and in some device one expert is named exactly 13 times.
All inputs are finite; a program needn't handle non-finite values.
Results may differ from a plain program's by a relative error of at most 0.012.
Values may be sent and summed in bfloat16 or wider, within the bound.
No kernel may reach another device: no remote copies, remote signals or barrier semaphores. Data moves between devices by JAX's collectives and lax.ppermute only.
A program may use at most 192 MiB of HBM per device.

v0:
```python
import jax
import jax.numpy as jnp
from jax import lax
from jax.sharding import PartitionSpec as P

D = 2048
HEADS = 16
NOPE = 128
ROPE = 64
LAT = 512
TOP = 6
PREF = 2
epsilon = 1e-06


def request_tables(lengths, request_ids, token_count):
    request_end = jnp.cumsum(lengths)
    positions = jnp.arange(token_count, dtype=jnp.int32)
    segment = jnp.sum((positions[:, None] >= request_end[None, :]).astype(jnp.int32), axis=1)
    matches = segment[:, None] == jnp.arange(request_ids.shape[0], dtype=jnp.int32)[None, :]
    prefix = jnp.sum(jnp.where(matches, request_ids[None, :], 0), axis=1)
    return (segment, prefix)


def split_kv(latent, w_ukv):
    row_count = latent.shape[0]
    joined = jnp.dot(latent, w_ukv, preferred_element_type=jnp.float32).astype(jnp.bfloat16)
    joined = joined.reshape(row_count, HEADS, 2 * NOPE).transpose(1, 0, 2)
    return (joined[:, :, :NOPE], joined[:, :, NOPE:])


def split_queries(query_rows):
    row_count = query_rows.shape[0]
    query_nope = query_rows[:, : HEADS * NOPE].reshape(row_count, HEADS, NOPE).transpose(1, 0, 2)
    query_rope = query_rows[:, HEADS * NOPE :].reshape(row_count, HEADS, ROPE).transpose(1, 0, 2)
    return (query_nope, query_rope)


def head_scores(head_nope, head_rope, head_keys, rope_keys):
    scaling = 1.0 / (NOPE + ROPE) ** 0.5
    content = lax.dot_general(
        head_nope, head_keys, (((1,), (1,)), ((), ())), preferred_element_type=jnp.float32
    )
    rotary = jnp.dot(head_rope, rope_keys, preferred_element_type=jnp.float32)
    return (content + rotary) * scaling


def block_partials(query_nope, query_rope, block_keys, block_values, rope_keys, allowed):

    def one_head(operands):
        head_nope, head_rope, head_keys, head_values = operands
        scores = jnp.where(
            allowed, head_scores(head_nope, head_rope, head_keys, rope_keys), -jnp.inf
        )
        maximum = jnp.max(scores, axis=1).astype(jnp.bfloat16)
        weights = jnp.where(allowed, jnp.exp(scores - maximum.astype(jnp.float32)[:, None]), 0.0)
        summed = jnp.sum(weights, axis=1).astype(jnp.bfloat16)
        weighted = jnp.dot(
            weights.astype(jnp.bfloat16), head_values, preferred_element_type=jnp.float32
        ).astype(jnp.bfloat16)
        return (weighted, maximum, summed)

    return lax.map(one_head, (query_nope, query_rope, block_keys, block_values))


def body(
    queries,
    suffix_latent,
    suffix_rope,
    residual,
    prefix_latent,
    prefix_rope,
    suffix_lengths,
    prefix_ids,
    w_ukv,
    w_out,
    norm_gain,
    expert_ids,
    gate_values,
    expert_gate_up,
    expert_down,
):
    token_count = queries.shape[0]
    req_count = lax.axis_size("req")
    wide_count = lax.axis_size("wide")
    segment, prefix = request_tables(suffix_lengths[0], prefix_ids[0], token_count)
    query_nope, query_rope = split_queries(queries)
    block_rows = prefix_latent.shape[2]
    key_owner = jnp.repeat(jnp.arange(PREF, dtype=jnp.int32), block_rows)
    group_prefix = lax.all_gather(prefix, "wide", axis=0, tiled=True)
    prefix_keys, prefix_values = split_kv(prefix_latent[0].reshape(PREF * block_rows, LAT), w_ukv)
    rope_keys = prefix_rope[0].transpose(1, 0, 2).reshape(ROPE, PREF * block_rows)
    piece_allowed = group_prefix[:, None] == key_owner[None, :]
    piece_nope, piece_rope = split_queries(lax.all_gather(queries, "wide", axis=0, tiled=True))
    remote_out, remote_max, remote_sum = block_partials(
        piece_nope, piece_rope, prefix_keys, prefix_values, rope_keys, piece_allowed
    )
    remote_out, remote_max, remote_sum = (
        lax.all_to_all(remote_out, "wide", split_axis=1, concat_axis=1, tiled=True),
        lax.all_to_all(remote_max, "wide", split_axis=1, concat_axis=1, tiled=True),
        lax.all_to_all(remote_sum, "wide", split_axis=1, concat_axis=1, tiled=True),
    )
    far_max = remote_max.astype(jnp.float32).reshape(HEADS, wide_count, token_count)
    far_sum = remote_sum.astype(jnp.float32).reshape(HEADS, wide_count, token_count)
    far_out = remote_out.reshape(HEADS, wide_count, token_count, NOPE)
    suffix_keys, suffix_values = split_kv(suffix_latent, w_ukv)
    positions = jnp.arange(token_count, dtype=jnp.int32)
    causal = (segment[:, None] == segment[None, :]) & (positions[None, :] <= positions[:, None])

    def local_head(operands):
        head_nope, head_rope, head_keys, head_values = operands
        scores = jnp.where(
            causal, head_scores(head_nope, head_rope, head_keys, suffix_rope), -jnp.inf
        )
        maximum = jnp.max(scores, axis=1)
        weights = jnp.where(causal, jnp.exp(scores - maximum[:, None]), 0.0)
        weighted = jnp.dot(
            weights.astype(jnp.bfloat16), head_values, preferred_element_type=jnp.float32
        )
        return (weighted, maximum, jnp.sum(weights, axis=1))

    local_out, local_max, local_sum = lax.map(
        local_head, (query_nope, query_rope, suffix_keys, suffix_values)
    )
    largest = jnp.maximum(local_max, jnp.max(far_max, axis=1))
    far_weight = jnp.exp(far_max - largest[:, None, :])
    near_weight = jnp.exp(local_max - largest)
    numerator = near_weight[:, :, None] * local_out + jnp.sum(
        far_weight[:, :, :, None] * far_out.astype(jnp.float32), axis=1
    )
    denominator = near_weight * local_sum + jnp.sum(far_weight * far_sum, axis=1)
    head_out = (numerator / denominator[:, :, None]).astype(jnp.bfloat16)
    attention = jnp.einsum(
        "htn,hnd->td", head_out, w_out.reshape(HEADS, NOPE, D), preferred_element_type=jnp.float32
    )
    hidden = (residual.astype(jnp.float32) + attention).astype(jnp.bfloat16)
    hidden_f32 = hidden.astype(jnp.float32)
    inverse = lax.rsqrt(jnp.mean(hidden_f32 * hidden_f32, axis=1, keepdims=True) + epsilon)
    normed = (hidden_f32 * inverse * norm_gain.astype(jnp.float32)[None, :]).astype(jnp.bfloat16)
    experts = req_count * wide_count // 2
    capacity = token_count * TOP // experts + 1
    flat_ids = expert_ids.reshape(-1)
    one_hot = (flat_ids[:, None] == jnp.arange(experts, dtype=jnp.int32)[None, :]).astype(jnp.int32)
    slot_index = jnp.sum((jnp.cumsum(one_hot, axis=0) - 1) * one_hot, axis=1)
    target = flat_ids * capacity + slot_index
    placement = jnp.arange(experts * capacity, dtype=jnp.int32)[:, None] == target[None, :]
    placed = placement.reshape(experts * capacity, token_count, TOP)
    dispatch_rows = jnp.any(placed, axis=2).astype(jnp.bfloat16)
    combine_rows = jnp.sum(jnp.where(placed, gate_values[None, :, :], 0.0), axis=2)
    outgoing = jnp.dot(dispatch_rows, normed, preferred_element_type=jnp.float32).astype(
        jnp.bfloat16
    )
    outgoing = outgoing.reshape(experts, capacity, D)
    doubled = jnp.broadcast_to(
        outgoing.reshape(experts, 1, capacity, D), (experts, 2, capacity, D)
    ).reshape(2 * experts, capacity, D)
    batch_in = lax.all_to_all(doubled, ("req", "wide"), split_axis=0, concat_axis=0, tiled=True)
    batch_shape = batch_in.shape
    flat_rows = batch_in.reshape(-1, D)
    gate_up = jnp.dot(flat_rows, expert_gate_up[0], preferred_element_type=jnp.float32)
    half_width = gate_up.shape[1] // 2
    activated = (jax.nn.silu(gate_up[:, :half_width]) * gate_up[:, half_width:]).astype(
        jnp.bfloat16
    )
    produced = jnp.dot(activated, expert_down[0], preferred_element_type=jnp.float32).astype(
        jnp.bfloat16
    )
    returned = lax.all_to_all(
        produced.reshape(batch_shape), ("req", "wide"), split_axis=0, concat_axis=0, tiled=True
    )
    halves = returned.reshape(experts, 2, capacity, D).astype(jnp.float32)
    summed_rows = (halves[:, 0] + halves[:, 1]).reshape(experts * capacity, D)
    mixture = lax.dot_general(
        combine_rows,
        summed_rows,
        (((0,), (0,)), ((), ())),
        precision=lax.Precision.HIGHEST,
        preferred_element_type=jnp.float32,
    )
    return (hidden_f32 + mixture).astype(jnp.bfloat16)


def solution(mesh):
    return jax.shard_map(
        body,
        mesh=mesh,
        in_specs=(
            P(("req", "wide"), None),
            P(("req", "wide"), None),
            P(None, ("req", "wide")),
            P(("req", "wide"), None),
            P("req", None, "wide", None),
            P("req", None, None, "wide"),
            P(("req", "wide"), None),
            P(("req", "wide"), None),
            P(),
            P(),
            P(),
            P(("req", "wide"), None),
            P(("req", "wide"), None),
            P(("req", "wide"), None, None),
            P(("req", "wide"), None, None),
        ),
        out_specs=P(("req", "wide"), None),
        check_vma=False,
    )
```

profile of v0, /device:TPU:37, one launch (start us, length us, event | category | flops | bytes accessed | tf_op | source)
XLA Modules:
  0.0 731.8 jit_solution(18404223918668810969)
XLA Ops:
  6.5 2.4 copy.133
  10.1 3.5 convolution_convert_fusion.2
  15.4 2.9 convolution_convert_fusion.3
  22.1 17.1 %all-gather = s32[16,1,128]{2,1,0:T(1,128)S(1)} all-gather(s32[1,1,128]{2,1,0:T(1,128)S(1)} %bitcast.195), channel_id=1, replica_groups=mesh['req'=8,'wide'=16] {'wide'}, dimensions={0}, use_global_device_ids=true | all-gather | bytes 8704 | tf_op jit(solution)/shard_map/all_gather | solution.py:90
  41.6 3.1 fusion.74
  44.7 62.2 %all-gather.3.cloned.1.call-done = bf16[2048,3072]{0,1:T(8,128)(2,1)} async-done(((bf16[128,3072]{0,1:T(8,128)(2,1)}), bf16[2048,3072]{0,1:T(8,128)(2,1)}) %all-gather.3.cloned.1.call-update) | async-done | bytes 12582928 | tf_op jit(solution)/shard_map/all_gather | solution.py:94
  106.9 8.2 %slice.60 = bf16[2048,2048]{0,1:T(8,128)(2,1)} slice(bf16[2048,3072]{0,1:T(8,128)(2,1)} %all-gather.3.cloned.1.call-done), slice={[0:2048], [0:2048]} | slice | bytes 16777216 | tf_op jit(solution)/shard_map/slice | solution.py:34
  115.2 4.7 slice.62
  119.9 98.8 %while.31 = (s32[]{:T(128)}, bf16[16,2048,128]{2,1,0:T(8,128)(2,1)}, bf16[16,2048]{1,0:T(8,128)(2,1)S(1)}, bf16[16,2048]{1,0:T(8,128)(2,1)S(1)}, bf16[16,2048,12...) while((s32[]{:T(128)}, ...), condition=%wide.region_10.11_spmd.clone, body=%wide.region_7.10_spmd.clone.sunk | while | flops 342620160 | bytes 12060293 | solution.py:63
  178.6 2.4 fusion.122
  219.4 6.4 all-to-all-start
  226.3 3.9 all-to-all-done
  230.3 5.4 all-to-all-start.2
  240.1 10.3 %copy.147 = bf16[16,2048,128]{2,0,1:T(8,128)(2,1)} copy(bf16[16,2048,128]{2,1,0:T(8,128)(2,1)} %get-tuple-element.116) | data formatting | bytes 16777216 | tf_op jit(solution)/shard_map/while | solution.py:63
  251.1 6.7 all-to-all-start.1
  257.7 136.6 %while.30 = (s32[]{:T(128)}, f32[16,128,128]{2,0,1:T(8,128)}, f32[16,128]{1,0:T(8,128)}, f32[16,128]{1,0:T(8,128)}, bf16[16,128,128]{1,2,0:T(8,128)(2,1)S(1)}, /...) while((s32[]{:T(128)}, f32[16,128,128]{2,0,1:T(8,128)}, ...), condition=%wide.region_5.6_spmd.clone, body=%wide.region_2.5_spmd.clone.sunk | while | flops 10796802 | bytes 664193 | solution.py:122
  260.6 3.0 dynamic_update_slice.35
  269.2 3.0 dynamic_update_slice.35
  277.7 3.0 dynamic_update_slice.35
  286.3 3.0 dynamic_update_slice.35
  294.8 3.0 dynamic_update_slice.35
  303.3 3.0 dynamic_update_slice.35
  311.9 3.0 dynamic_update_slice.35
  320.4 3.0 dynamic_update_slice.35
  329.0 3.0 dynamic_update_slice.35
  337.5 3.0 dynamic_update_slice.35
  346.0 3.0 dynamic_update_slice.35
  354.6 3.0 dynamic_update_slice.35
  363.1 3.0 dynamic_update_slice.35
  371.6 3.0 dynamic_update_slice.35
  380.2 3.0 dynamic_update_slice.35
  388.7 3.0 dynamic_update_slice.35
  399.1 6.6 fusion.52
  406.5 4.8 multiply_reduce_fusion
  412.4 2.9 convolution_convert_fusion.4
  415.3 5.0 broadcast_in_dim.103
  420.3 6.8 broadcast_in_dim.104
  427.0 107.6 %all_to_all.33 = bf16[128,13,2048]{2,1,0:T(8,128)(2,1)} all-to-all(bf16[128,13,2048]{2,1,0:T(8,128)(2,1)} %bitcast.180), channel_id=1, replica_groups=mesh['req'=8,'wide'=16] {'req','wide'}, dimensions={0} | all-to-all | bytes 13631488 | tf_op jit(solution)/shard_map/all_to_all | solution.py:157
  534.6 9.3 %reshape.162 = bf16[1664,2048]{1,0:T(8,128)(2,1)} reshape(bf16[128,13,2048]{2,1,0:T(8,128)(2,1)} %all_to_all.33) | data formatting | bytes 13631488 | tf_op jit(solution)/shard_map/reshape | solution.py:159
  543.9 15.1 %fusion.54 = f32[1664,1408]{0,1:T(8,128)S(1)} fusion(bf16[1664,2048]{1,0:T(8,128)(2,1)} %reshape.162, bf16[1,2048,1408]{2,1,0:T(8,128)(2,1)} %param.32), kind=kOutput, calls=%fused_computation.60 | convolution fusion | flops 9596567552 | bytes 21954560 | tf_op jit(solution)/shard_map/dot_general | solution.py:160
  559.0 7.8 %convolution_convert_fusion.1 = bf16[1664,2048]{1,0:T(8,128)(2,1)} fusion(bf16[1,704,2048]{2,1,0:T(8,128)(2,1)S(1)} %copy-done, f32[1664,1408]{0,1:T(8,128)S(1)} %fusion.54), kind=kOutput, calls=%fused_computation.59 | convolution fusion | flops 4808720384 | bytes 19070976 | tf_op jit(solution)/shard_map/dot_general | solution.py:165
  566.8 9.1 %reshape.163 = bf16[128,13,2048]{2,1,0:T(8,128)(2,1)} reshape(bf16[1664,2048]{1,0:T(8,128)(2,1)} %convolution_convert_fusion.1) | data formatting | bytes 13631488 | tf_op jit(solution)/shard_map/reshape | solution.py:169
  575.9 8.5 %all-to-all-start.4 = ((bf16[128,13,2048]{2,1,0:T(8,128)(2,1)}), bf16[128,13,2048]{2,1,0:T(8,128)(2,1)}, u32[]{:S(2)}, u32[]{:S(2)}) async-start(bf16[128,13,2048]{2,1,0:T(8,128)(2,1)} %reshape.163), calls=%async_computation.4 | async-start | bytes 16777216 | tf_op jit(solution)/shard_map/all_to_all | solution.py:168
  584.7 103.2 %all-to-all-done.4 = bf16[128,13,2048]{2,1,0:T(8,128)(2,1)} async-done(((bf16[128,13,2048]{2,1,0:T(8,128)(2,1)}), bf16[128,13,2048]{2,1,0:T(8,128)(2,1)}, u32[]{:S(2)}, u32[]{:S(2)}) %all-to-all-start.4) | async-done | bytes 6815776 | tf_op jit(solution)/shard_map/all_to_all | solution.py:168
  687.9 11.2 %convert.4 = f32[64,2,13,2048]{3,2,1,0:T(8,128)} convert(bf16[64,2,13,2048]{3,2,1,0:T(8,128)(2,1)} %bitcast.27) | non-fusion elementwise | flops 3407872 | bytes 20447232 | tf_op jit(solution)/shard_map/convert_element_type | solution.py:171
  699.2 11.7 %fusion.53 = f32[64,1,13,2048]{3,2,0,1:T(8,128)} fusion(f32[64,2,13,2048]{3,2,1,0:T(8,128)} %convert.4), kind=kLoop, calls=%fused_computation.57 | loop fusion | flops 1703936 | bytes 20447232 | tf_op jit(solution)/shard_map/add | solution.py:172
  710.9 6.8 add.64
  717.6 7.3 fusion.62
  (314 shorter events, 206.5 us)
Async XLA Ops:
  6.5 552.4 %copy-start = (bf16[1,704,2048]{2,1,0:T(8,128)(2,1)S(1)}, bf16[1,704,2048]{2,1,0:T(8,128)(2,1)}, u32[]{:S(2)}) copy-start(bf16[1,704,2048]{2,1,0:T(8,128)(2,1)} %param.33) | copy-start | bytes 8650756
  6.5 100.4 %all-gather.3.cloned.1.call-start = ((), (), s32[]{:S(2)}) async-start(), calls=%async_computation.5 | async-start | bytes 13369344 | tf_op jit(solution)/shard_map/all_gather | solution.py:94
  13.7 1.6 copy-start.13
  13.7 1.8 copy-start.7
  15.4 6.6 copy-start.14
  15.4 23.9 %copy-start.10 = (s32[128,6]{0,1:T(8,128)S(1)}, s32[128,6]{0,1:T(8,128)}, u32[]{:S(2)}) copy-start(s32[128,6]{0,1:T(8,128)} %param.30) | copy-start | bytes 9220
  15.4 23.9 %copy-start.9 = (bf16[1,2,64,128]{3,2,1,0:T(8,128)(2,1)S(1)}, bf16[1,2,64,128]{3,2,1,0:T(8,128)(2,1)}, u32[]{:S(2)}) copy-start(bf16[1,2,64,128]{3,2,1,0:T(8,128)(2,1)} %param.24) | copy-start | bytes 98308
  119.9 119.6 %copy-start.12 = (bf16[2048]{0:T(1024)(128)(2,1)S(1)}, bf16[2048]{0:T(1024)(128)(2,1)}, u32[]{:S(2)}) copy-start(bf16[2048]{0:T(1024)(128)(2,1)} %param.29) | copy-start | bytes 12292
  219.4 10.9 %all-to-all-start = ((bf16[16,16,128]{2,0,1:T(8,128)(2,1)}), bf16[16,16,128]{2,0,1:T(8,128)(2,1)S(1)}, u32[]{:S(2)}, u32[]{:S(2)}) async-start(bf16[16,16,128]{2,0,1:T(8,128)(2,1)} %copy_bitcast_fusion.1), calls=%async_computation | async-start | bytes 131072 | tf_op jit(solution)/shard_map/all_to_all | solution.py:100
  230.3 20.1 %copy-start.4 = (bf16[16,16,128]{2,0,1:T(8,128)(2,1)}, bf16[16,16,128]{2,0,1:T(8,128)(2,1)S(1)}, u32[]{:S(2)}) copy-start(bf16[16,16,128]{2,0,1:T(8,128)(2,1)S(1)} %all-to-all-done) | copy-start | bytes 196612
  230.3 20.1 %all-to-all-start.2 = ((bf16[16,16,128]{2,0,1:T(8,128)(2,1)}), bf16[16,16,128]{2,0,1:T(8,128)(2,1)S(1)}, u32[]{:S(2)}, u32[]{:S(2)}) async-start(bf16[16,16,128]{2,0,1:T(8,128)(2,1)} %copy_bitcast_fusion), calls=%async_computation.2 | async-start | bytes 131072 | tf_op jit(solution)/shard_map/all_to_all | solution.py:101
  250.4 0.6 copy-start.6
  251.1 148.1 %all-to-all-start.1 = ((bf16[16,2048,128]{2,0,1:T(8,128)(2,1)}), bf16[16,2048,128]{2,0,1:T(8,128)(2,1)}, u32[]{:S(2)}, u32[]{:S(2)}) async-start(bf16[16,2048,128]{2,0,1:T(8,128)(2,1)} %copy.147), calls=%async_computation.1 | async-start | bytes 16777216 | tf_op jit(solution)/shard_map/all_to_all | solution.py:99
  399.1 6.6 copy-start.2
  399.1 7.3 %copy-start.5 = (bf16[128,2048]{1,0:T(8,128)(2,1)S(1)}, bf16[128,2048]{1,0:T(8,128)(2,1)}, u32[]{:S(2)}) copy-start(bf16[128,2048]{1,0:T(8,128)(2,1)} %param.22) | copy-start | bytes 1572868
  406.5 5.9 copy-start.3
  406.5 5.9 copy-start.8
  411.4 1.1 copy-start.1
  575.8 8.5 %copy-start.11 = (f32[128,6]{0,1:T(8,128)S(1)}, f32[128,6]{0,1:T(8,128)}, u32[]{:S(2)}) copy-start(f32[128,6]{0,1:T(8,128)} %param.31) | copy-start | bytes 9220
  575.9 112.1 %all-to-all-start.4 = ((bf16[128,13,2048]{2,1,0:T(8,128)(2,1)}), bf16[128,13,2048]{2,1,0:T(8,128)(2,1)}, u32[]{:S(2)}, u32[]{:S(2)}) async-start(bf16[128,13,2048]{2,1,0:T(8,128)(2,1)} %reshape.163), calls=%async_computation.4 | async-start | bytes 16777216 | tf_op jit(solution)/shard_map/all_to_all | solution.py:168
Sparse Core Ops, SparseCore 0:
  9.4 97.4 all-gather.2
where the time goes:
time: 739 us; the launch traced here: 732 us
  matrix products  177 us (24%)
  local copies, waits for them, and re-layouts  172 us (23%)
  waiting for transfers between devices  169 us (23%)
  blocking collectives  125 us (17%)
  other arithmetic  46.8 us (6%)
  starting transfers between devices  26.9 us (4%)
  between operations  13.7 us (2%)
    all_to_all x1, blocking collectives, body(): lax.all_to_all(doubled, ('req', 'wide'), split_axis=0, concat_axis=0, til...  108 us
    all_to_all x1, waiting for transfers between devices, body(): lax.all_to_all(produced.reshape(batch_shape), ('req', 'wide'), split_axis...  103 us
    dynamic_update_slice x48, local copies, waits for them, and re-layouts, body(): lax.map(local_head, (query_nope, query_rope, suffix_keys, suffix_values))  88.7 us
    all_gather x1, waiting for transfers between devices, body(): lax.all_gather(queries, 'wide', axis=0, tiled=True)  62.2 us
    dot_general x32, matrix products, head_scores(): rotary = jnp.dot(head_rope, rope_keys, preferred_element_type=jnp.float32)  39.9 us
    dot_general x32, matrix products, head_scores(): lax.dot_general(head_nope, head_keys, (((1,), (1,)), ((), ())), preferred...  38.9 us
    dot_general x16, matrix products, one_head(): jnp.dot(weights.astype(jnp.bfloat16), head_values, preferred_element_type...  37.5 us
    all_gather x1, blocking collectives, body(): group_prefix = lax.all_gather(prefix, 'wide', axis=0, tiled=True)  17.1 us
  transfers between devices with their start and end apart: 5, of which 3 were waited for; matrix products, arithmetic and copies ran while one was open for 24% of the time, Pallas kernels for 0%

commit v1 on v0

--- a/solution.py
+++ b/solution.py
@@ -91,7 +91,11 @@
     prefix_keys, prefix_values = split_kv(prefix_latent[0].reshape(PREF * block_rows, LAT), w_ukv)
     rope_keys = prefix_rope[0].transpose(1, 0, 2).reshape(ROPE, PREF * block_rows)
     piece_allowed = group_prefix[:, None] == key_owner[None, :]
-    piece_nope, piece_rope = split_queries(lax.all_gather(queries, "wide", axis=0, tiled=True))
+    piece_nope, piece_rope = split_queries(
+        jnp.concatenate(
+            lax.all_to_all(jnp.stack([queries] * lax.axis_size("wide")), "wide", 0, 0), axis=0
+        )
+    )
     remote_out, remote_max, remote_sum = block_partials(
         piece_nope, piece_rope, prefix_keys, prefix_values, rope_keys, piece_allowed
     )

time: 739 us -> 891 us (1.21)
  blocking collectives: 125 us -> 328 us
  waiting for transfers between devices: 169 us -> 107 us
  local copies, waits for them, and re-layouts: 172 us -> 189 us
  between operations: 13.7 us -> 0.26 us
    all_gather x1, blocking collectives: 17.1 us -> 216 us  [body(): group_prefix = lax.all_gather(prefix, 'wide', axis=0, tiled=True)]
    all_gather x1 -> x0, waiting for transfers between devices: 62.2 us -> none  [body(): lax.all_gather(queries, 'wide', axis=0, tiled=True)]
    reshape x0 -> x1, local copies, waits for them, and re-layouts: none -> 10.9 us  [body(): jnp.concatenate(lax.all_to_all(jnp.stack([queries] * lax.axis_size('wide'...]
  transfers between devices with their start and end apart: 5 -> 5, of which waited for: 3 -> 2; matrix products, arithmetic and copies ran while one was open for 24% -> 20% of each run, Pallas kernels for 0% -> 0%
where the time goes in v1:
time: 891 us; the launch traced here: 883 us
  blocking collectives  328 us (37%)
  local copies, waits for them, and re-layouts  189 us (21%)
  matrix products  177 us (20%)
  waiting for transfers between devices  107 us (12%)
  other arithmetic  46.8 us (5%)
  starting transfers between devices  34 us (4%)
    all_gather x1, blocking collectives, body(): group_prefix = lax.all_gather(prefix, 'wide', axis=0, tiled=True)  216 us
    all_to_all x1, blocking collectives, body(): lax.all_to_all(doubled, ('req', 'wide'), split_axis=0, concat_axis=0, til...  111 us
    all_to_all x1, waiting for transfers between devices, body(): lax.all_to_all(produced.reshape(batch_shape), ('req', 'wide'), split_axis...  103 us
    dynamic_update_slice x48, local copies, waits for them, and re-layouts, body(): lax.map(local_head, (query_nope, query_rope, suffix_keys, suffix_values))  88.6 us
    dot_general x32, matrix products, head_scores(): rotary = jnp.dot(head_rope, rope_keys, preferred_element_type=jnp.float32)  39.9 us
    dot_general x32, matrix products, head_scores(): lax.dot_general(head_nope, head_keys, (((1,), (1,)), ((), ())), preferred...  38.9 us
    dot_general x16, matrix products, one_head(): jnp.dot(weights.astype(jnp.bfloat16), head_values, preferred_element_type...  37.5 us
  transfers between devices with their start and end apart: 5, of which 2 were waited for; matrix products, arithmetic and copies ran while one was open for 20% of the time, Pallas kernels for 0%

profile of v1, /device:TPU:37, one launch (start us, length us, event | category | flops | bytes accessed | tf_op | source)
XLA Modules:
  0.0 883.3 jit_solution(5328446779660520221)
XLA Ops:
  2.5 8.0 stack.2
  10.5 7.0 all-to-all-start
  18.0 3.6 convolution_convert_fusion.2
  23.2 2.9 convolution_convert_fusion.3
  29.9 216.2 %all-gather = s32[16,1,128]{2,1,0:T(1,128)S(1)} all-gather(s32[1,1,128]{2,1,0:T(1,128)S(1)} %bitcast.200), channel_id=1, replica_groups=mesh['req'=8,'wide'=16] {'wide'}, dimensions={0}, use_global_device_ids=true | all-gather | bytes 8704 | tf_op jit(solution)/shard_map/all_gather | solution.py:90
  248.4 3.1 fusion.74
  251.6 10.9 %copy_bitcast_fusion = bf16[2048,3072]{0,1:T(8,128)(2,1)} fusion(bf16[16,128,3072]{1,2,0:T(8,128)(2,1)} %all-to-all-done), kind=kLoop, calls=%fused_computation.56 | loop fusion | bytes 25165824 | tf_op jit(solution)/shard_map/reshape | solution.py:95
  262.4 8.3 slice.60
  270.7 4.7 slice.62
  275.4 98.8 %while.31 = (s32[]{:T(128)}, bf16[16,2048,128]{2,1,0:T(8,128)(2,1)}, bf16[16,2048]{1,0:T(8,128)(2,1)S(1)}, bf16[16,2048]{1,0:T(8,128)(2,1)S(1)}, bf16[16,2048,12...) while((s32[]{:T(128)}, ...), condition=%wide.region_10.11_spmd.clone, body=%wide.region_7.10_spmd.clone.sunk | while | flops 342620160 | bytes 12060293 | solution.py:63
  374.9 6.4 all-to-all-start.1
  382.0 3.9 all-to-all-done.1
  385.9 5.4 all-to-all-start.3
  394.6 10.3 %copy.152 = bf16[16,2048,128]{2,0,1:T(8,128)(2,1)} copy(bf16[16,2048,128]{2,1,0:T(8,128)(2,1)} %get-tuple-element.116) | data formatting | bytes 16777216 | tf_op jit(solution)/shard_map/while | solution.py:63
  405.6 6.7 all-to-all-start.2
  412.3 136.5 %while.30 = (s32[]{:T(128)}, f32[16,128,128]{2,0,1:T(8,128)}, f32[16,128]{1,0:T(8,128)}, f32[16,128]{1,0:T(8,128)}, bf16[16,128,128]{1,2,0:T(8,128)(2,1)S(1)}, /...) while((s32[]{:T(128)}, f32[16,128,128]{2,0,1:T(8,128)}, ...), condition=%wide.region_5.6_spmd.clone, body=%wide.region_2.5_spmd.clone.sunk | while | flops 10796802 | bytes 664193 | solution.py:126
  415.2 3.0 dynamic_update_slice.35
  423.7 3.0 dynamic_update_slice.35
  432.2 3.0 dynamic_update_slice.35
  440.8 3.0 dynamic_update_slice.35
  449.3 3.0 dynamic_update_slice.35
  457.8 3.0 dynamic_update_slice.35
  466.4 3.0 dynamic_update_slice.35
  474.9 3.0 dynamic_update_slice.35
  483.4 3.0 dynamic_update_slice.35
  492.0 3.0 dynamic_update_slice.35
  500.5 3.0 dynamic_update_slice.35
  509.0 3.0 dynamic_update_slice.35
  517.6 3.0 dynamic_update_slice.35
  526.1 3.0 dynamic_update_slice.35
  534.6 3.0 dynamic_update_slice.35
  543.1 3.0 dynamic_update_slice.35
  553.6 6.6 fusion.52
  560.9 4.8 multiply_reduce_fusion
  566.9 2.9 convolution_convert_fusion.4
  569.7 5.0 broadcast_in_dim.103
  574.7 6.8 broadcast_in_dim.104
  581.5 111.5 %all_to_all.38 = bf16[128,13,2048]{2,1,0:T(8,128)(2,1)} all-to-all(bf16[128,13,2048]{2,1,0:T(8,128)(2,1)} %bitcast.185), channel_id=1, replica_groups=mesh['req'=8,'wide'=16] {'req','wide'}, dimensions={0} | all-to-all | bytes 13631488 | tf_op jit(solution)/shard_map/all_to_all | solution.py:161
  692.9 9.3 %reshape.168 = bf16[1664,2048]{1,0:T(8,128)(2,1)} reshape(bf16[128,13,2048]{2,1,0:T(8,128)(2,1)} %all_to_all.38) | data formatting | bytes 13631488 | tf_op jit(solution)/shard_map/reshape | solution.py:163
  702.2 15.1 %fusion.54 = f32[1664,1408]{0,1:T(8,128)S(1)} fusion(bf16[1664,2048]{1,0:T(8,128)(2,1)} %reshape.168, bf16[1,2048,1408]{2,1,0:T(8,128)(2,1)} %param.32), kind=kOutput, calls=%fused_computation.61 | convolution fusion | flops 9596567552 | bytes 21954560 | tf_op jit(solution)/shard_map/dot_general | solution.py:164
  717.3 7.8 convolution_convert_fusion.1
  725.1 9.1 %reshape.169 = bf16[128,13,2048]{2,1,0:T(8,128)(2,1)} reshape(bf16[1664,2048]{1,0:T(8,128)(2,1)} %convolution_convert_fusion.1) | data formatting | bytes 13631488 | tf_op jit(solution)/shard_map/reshape | solution.py:173
  734.2 8.5 all-to-all-start.5
  743.0 103.2 %all-to-all-done.5 = bf16[128,13,2048]{2,1,0:T(8,128)(2,1)} async-done(((bf16[128,13,2048]{2,1,0:T(8,128)(2,1)}), bf16[128,13,2048]{2,1,0:T(8,128)(2,1)}, u32[]{:S(2)}, u32[]{:S(2)}) %all-to-all-start.5) | async-done | bytes 6815776 | tf_op jit(solution)/shard_map/all_to_all | solution.py:172
  846.3 11.2 %convert.4 = f32[64,2,13,2048]{3,2,1,0:T(8,128)} convert(bf16[64,2,13,2048]{3,2,1,0:T(8,128)(2,1)} %bitcast.27) | non-fusion elementwise | flops 3407872 | bytes 20447232 | tf_op jit(solution)/shard_map/convert_element_type | solution.py:175
  857.5 11.7 %fusion.53 = f32[64,1,13,2048]{3,2,0,1:T(8,128)} fusion(f32[64,2,13,2048]{3,2,1,0:T(8,128)} %convert.4), kind=kLoop, calls=%fused_computation.58 | loop fusion | flops 1703936 | bytes 20447232 | tf_op jit(solution)/shard_map/add | solution.py:176
  869.2 6.8 add.64
  876.0 7.3 fusion.62
  (316 shorter events, 209.5 us)
Async XLA Ops:
  0.0 717.3 %copy-start = (bf16[1,704,2048]{2,1,0:T(8,128)(2,1)S(1)}, bf16[1,704,2048]{2,1,0:T(8,128)(2,1)}, u32[]{:S(2)}) copy-start(bf16[1,704,2048]{2,1,0:T(8,128)(2,1)} %param.33) | copy-start | bytes 8650756
  10.5 7.1 copy-start.10
  10.5 241.1 %all-to-all-start = ((bf16[16,128,3072]{1,2,0:T(8,128)(2,1)}), bf16[16,128,3072]{1,2,0:T(8,128)(2,1)}, u32[]{:S(2)}, u32[]{:S(2)}) async-start(bf16[16,128,3072]{1,2,0:T(8,128)(2,1)} %stack.2), calls=%async_computation | async-start | bytes 25165824 | tf_op jit(solution)/shard_map/all_to_all | solution.py:96
  17.9 5.1 copy-start.13
  17.9 5.3 copy-start.7
  23.1 6.7 copy-start.14
  23.1 223.0 %copy-start.9 = (bf16[1,2,64,128]{3,2,1,0:T(8,128)(2,1)S(1)}, bf16[1,2,64,128]{3,2,1,0:T(8,128)(2,1)}, u32[]{:S(2)}) copy-start(bf16[1,2,64,128]{3,2,1,0:T(8,128)(2,1)} %param.24) | copy-start | bytes 98308
  275.4 118.5 %copy-start.12 = (bf16[2048]{0:T(1024)(128)(2,1)S(1)}, bf16[2048]{0:T(1024)(128)(2,1)}, u32[]{:S(2)}) copy-start(bf16[2048]{0:T(1024)(128)(2,1)} %param.29) | copy-start | bytes 12292
  374.9 11.0 %all-to-all-start.1 = ((bf16[16,16,128]{2,0,1:T(8,128)(2,1)}), bf16[16,16,128]{2,0,1:T(8,128)(2,1)S(1)}, u32[]{:S(2)}, u32[]{:S(2)}) async-start(bf16[16,16,128]{2,0,1:T(8,128)(2,1)} %copy_bitcast_fusion.2), calls=%async_computation.1 | async-start | bytes 131072 | tf_op jit(solution)/shard_map/all_to_all | solution.py:104
  385.9 19.0 %copy-start.4 = (bf16[16,16,128]{2,0,1:T(8,128)(2,1)}, bf16[16,16,128]{2,0,1:T(8,128)(2,1)S(1)}, u32[]{:S(2)}) copy-start(bf16[16,16,128]{2,0,1:T(8,128)(2,1)S(1)} %all-to-all-done.1) | copy-start | bytes 196612
  385.9 19.0 %all-to-all-start.3 = ((bf16[16,16,128]{2,0,1:T(8,128)(2,1)}), bf16[16,16,128]{2,0,1:T(8,128)(2,1)S(1)}, u32[]{:S(2)}, u32[]{:S(2)}) async-start(bf16[16,16,128]{2,0,1:T(8,128)(2,1)} %copy_bitcast_fusion.1), calls=%async_computation.3 | async-start | bytes 131072 | tf_op jit(solution)/shard_map/all_to_all | solution.py:105
  404.9 7.3 slice-start
  404.9 0.6 copy-start.6
  405.6 148.0 %all-to-all-start.2 = ((bf16[16,2048,128]{2,0,1:T(8,128)(2,1)}), bf16[16,2048,128]{2,0,1:T(8,128)(2,1)}, u32[]{:S(2)}, u32[]{:S(2)}) async-start(bf16[16,2048,128]{2,0,1:T(8,128)(2,1)} %copy.152), calls=%async_computation.2 | async-start | bytes 16777216 | tf_op jit(solution)/shard_map/all_to_all | solution.py:103
  553.6 6.6 copy-start.2
  553.6 7.3 copy-start.5
  560.9 5.9 copy-start.3
  560.9 5.9 copy-start.8
  565.8 1.1 copy-start.1
  734.2 8.5 copy-start.11
  734.2 112.1 %all-to-all-start.5 = ((bf16[128,13,2048]{2,1,0:T(8,128)(2,1)}), bf16[128,13,2048]{2,1,0:T(8,128)(2,1)}, u32[]{:S(2)}, u32[]{:S(2)}) async-start(bf16[128,13,2048]{2,1,0:T(8,128)(2,1)} %reshape.169), calls=%async_computation.5 | async-start | bytes 16777216 | tf_op jit(solution)/shard_map/all_to_all | solution.py:172
